TPU v7x, 256 devices: a whole 4x4x8 slice. The times are simulated.
256 devices in a mesh: leaf: 32 (over y, z), panel: 8 (over x, core).
Axes of the slice: x: 4, y: 4, z: 8, core: 2. Of those that a mesh axis runs over, the one named last changes fastest.
Arguments:
- child_front: float32 [32, 2, 8, 128, 2048], P('leaf', None, 'panel'), as said below
- parent_entries: float32 [32, 4, 8, 128, 512], P('leaf', None, 'panel'), as said below
- parent_of: int32 [32], replicated, may hold values from 0 to 31
- owner_slot: int32 [32], replicated, may hold values from 0 to 31, each once
- front_blocks: int32 [32], replicated, may hold values from 8 to 32, as said below
- block_lists: int32 [32, 8], replicated, may hold values from 0 to 31, as said below
Outputs:
- child_factor: float32 [32, 2, 8, 128, 1024], P('leaf', None, 'panel')
- parent_factor: float32 [32, 4, 8, 128, 512], P('leaf', None, 'panel')
Inputs may be any that keep to these rules, and one draw needn't show every extreme that they name: `front_blocks`: each entry is a multiple of the panel axis size; the largest equals 32. `block_lists`: the entries of a row are distinct, each below front_blocks of the child's parent, and entry k leaves the same remainder as k when divided by the panel axis size. `child_front`: symmetric, with a positive definite leading block of every front. `parent_entries`: the leading 512 rows form a symmetric positive definite block.
All inputs are finite; a program needn't handle non-finite values.
Results may differ from a plain program's by a relative error of at most 0.00044.
Values may be sent and summed in bfloat16 or wider, within the bound.
No kernel may reach another device: no remote copies, remote signals or barrier semaphores. Data moves between devices by JAX's collectives and lax.ppermute only.
A program may use at most 128 MiB of HBM per device.

v0:
```python
import jax
import jax.numpy as jnp
from jax import lax
from jax.sharding import PartitionSpec as P

BLK = 128
PANEL = 512
WC = 2048
PC = 1024
CBB = 8


def place_columns(block_rows, block_map):
    count_in = block_rows.shape[0]
    row_slots = block_rows.shape[1]
    pivot_blocks = PANEL // BLK
    onehot = (block_map[:, :, None] == jnp.arange(pivot_blocks)[None, None, :]).astype(jnp.bfloat16)
    split_blocks = block_rows.reshape(count_in, row_slots, BLK, CBB, BLK)
    placed = jnp.einsum(
        "muvkc,mkb->muvbc", split_blocks, onehot, preferred_element_type=jnp.float32
    )
    return placed.reshape(count_in, row_slots, BLK, PANEL)


def place_rows(assembled, placed, block_map, destination, panel_count, panel_index, leaf_index):
    count_in = placed.shape[0]
    row_slots = placed.shape[1]
    parent_slots = assembled.shape[0]
    grouped = block_map.reshape(count_in, row_slots, panel_count)
    pick = (jnp.arange(panel_count) == panel_index).astype(jnp.int32)
    row_blocks = jnp.sum(grouped * pick[None, None, :], axis=2)
    target = row_blocks[:, :, None] // panel_count == jnp.arange(parent_slots)[None, None, :]
    target = jnp.logical_and(target, (destination == leaf_index)[:, None, None]).astype(jnp.float32)
    return assembled + jnp.einsum("muvx,mut->tvx", placed, target, precision=lax.Precision.HIGHEST)


def on_device(child_front, parent_entries, parent_of, owner_slot, front_blocks, block_lists):
    panel_count = lax.axis_size("panel")
    panel_index = lax.axis_index("panel")
    leaf_index = lax.axis_index("leaf")
    row_slots = child_front.shape[1]
    parent_slots = parent_entries.shape[1]
    local_rows = child_front.reshape(row_slots * BLK, WC)
    factors = []
    for first_col in range(0, PC, PANEL):
        trailing = first_col + PANEL
        column = local_rows[:, first_col:trailing]
        gathered = lax.all_gather(
            column.reshape(row_slots, 1, BLK, PANEL), "panel", axis=1, tiled=True
        )
        gathered = gathered.reshape(WC, PANEL)
        pivot_block = jnp.linalg.cholesky(gathered[first_col:trailing])
        all_rows = jax.scipy.linalg.solve_triangular(pivot_block, gathered.T, lower=True).T
        all_rows = jnp.where(jnp.arange(WC)[:, None] >= first_col, all_rows, 0.0)
        own_rows = lax.dynamic_slice_in_dim(
            all_rows.reshape(row_slots, panel_count, BLK, PANEL), panel_index, 1, 1
        )
        own_rows = own_rows.reshape(row_slots * BLK, PANEL)
        update = jnp.dot(own_rows, all_rows[trailing:].T, precision=lax.Precision.HIGHEST)
        local_rows = jnp.concatenate(
            [local_rows[:, :trailing], local_rows[:, trailing:] - update], axis=1
        )
        factors.append(own_rows)
    child_factor = jnp.concatenate(factors, axis=1).reshape(1, row_slots, 1, BLK, PC)
    first_cb = PC // (BLK * panel_count)
    contribution = local_rows.reshape(row_slots, BLK, WC)[first_cb:, :, PC:].astype(jnp.bfloat16)
    parent_hits = (parent_of[:, None] == jnp.arange(owner_slot.shape[0])[None, :]).astype(jnp.int32)
    slot_of_child = jnp.sum(parent_hits * owner_slot[None, :], axis=1)
    live_mine = jnp.sum(jnp.where(owner_slot == leaf_index, front_blocks, 0))
    entries = parent_entries.reshape(parent_slots, BLK, PANEL)
    global_block = jnp.arange(parent_slots) * panel_count + panel_index
    initial = jnp.where((global_block < live_mine)[:, None, None], entries, 0.0)
    placed = place_columns(
        lax.all_gather(contribution[None], "leaf", axis=0, tiled=True), block_lists
    )
    assembled = place_rows(
        initial, placed, block_lists, slot_of_child, panel_count, panel_index, leaf_index
    )
    stacked = lax.all_gather(assembled[0], "panel", axis=0, tiled=True)
    pivot_block = jnp.linalg.cholesky(stacked[:PANEL])
    parent_rows = assembled.reshape(parent_slots * BLK, PANEL)
    parent_factor = jax.scipy.linalg.solve_triangular(pivot_block, parent_rows.T, lower=True).T
    return (child_factor, parent_factor.reshape(1, parent_slots, 1, BLK, PANEL))


def solution(mesh):
    in_specs = (
        P("leaf", None, "panel", None, None),
        P("leaf", None, "panel", None, None),
        P(),
        P(),
        P(),
        P(),
    )
    out_specs = (P("leaf", None, "panel", None, None), P("leaf", None, "panel", None, None))
    return jax.shard_map(
        on_device, mesh=mesh, in_specs=in_specs, out_specs=out_specs, check_vma=False
    )
```

profile of v0, /device:TPU:1, one launch (start us, length us, event | category | flops | bytes accessed | tf_op | source)
XLA Modules:
  0.0 736.7 jit_solution(10436099563935229929)
XLA Ops:
  9.2 40.2 %all-gather.7.cloned.1.call-done = f32[2,8,128,512]{3,2,0,1:T(8,128)} async-done(((f32[2,1,128,512]{3,2,0,1:T(8,128)}), f32[2,8,128,512]{3,2,0,1:T(8,128)}) %all-gather.7.cloned.1.call-update) | async-done | bytes 4194320 | tf_op jit(solution)/shard_map/all_gather | solution.py:48
  62.7 11.7 %cholesky.374 = f32[128,128]{1,0:T(8,128)S(1)} custom-call(f32[128,128]{1,0:T(8,128)S(1)} %cholesky.586), custom_call_target="Cholesky" | custom-call | tf_op jit(solution)/shard_map/jit(cholesky)/cholesky | solution.py:52
  85.1 11.9 %cholesky.393 = f32[128,128]{1,0:T(8,128)S(1)} custom-call(f32[128,128]{1,0:T(8,128)S(1)} %cholesky.590), custom_call_target="Cholesky" | custom-call | tf_op jit(solution)/shard_map/jit(cholesky)/cholesky | solution.py:52
  97.0 9.8 %custom-call.36 = f32[1,128,128]{1,2,0:T(8,128)S(1)} custom-call(f32[1,128,128]{2,1,0:T(8,128)S(1)} %get-tuple-element.100), custom_call_target="InvertDiagBlocksLowerTriangular" | custom-call | tf_op jit(solution)/shard_map/jit(cholesky)/cholesky | solution.py:52
  107.5 11.7 %cholesky.414 = f32[128,128]{1,0:T(8,128)S(1)} custom-call(f32[128,128]{1,0:T(8,128)S(1)} %cholesky.595), custom_call_target="Cholesky" | custom-call | tf_op jit(solution)/shard_map/jit(cholesky)/cholesky | solution.py:52
  130.3 12.1 %cholesky.431 = f32[128,128]{1,0:T(8,128)S(1)} custom-call(f32[128,128]{1,0:T(8,128)S(1)} %convolution_subtract_fusion.15), custom_call_target="Cholesky" | custom-call | tf_op jit(solution)/shard_map/jit(cholesky)/cholesky | solution.py:52
  154.5 39.3 %custom-call.38 = f32[4,128,128]{1,2,0:T(8,128)S(1)} custom-call(f32[4,128,128]{2,1,0:T(8,128)S(1)} %get-tuple-element.26), custom_call_target="InvertDiagBlocksLowerTriangular" | custom-call | tf_op jit(solution)/shard_map/jit(_solve_triangular)/triangular_solve | solution.py:53
  213.6 33.6 %all-gather.9.cloned.1.call-done = f32[2,8,128,512]{3,2,0,1:T(8,128)} async-done(((f32[2,1,128,512]{3,2,0,1:T(8,128)}), f32[2,8,128,512]{3,2,0,1:T(8,128)}) %all-gather.9.cloned.1.call-update) | async-done | bytes 4194320 | tf_op jit(solution)/shard_map/all_gather | solution.py:48
  263.9 11.7 %cholesky.446 = f32[128,128]{1,0:T(8,128)S(1)} custom-call(f32[128,128]{1,0:T(8,128)S(1)} %cholesky.599), custom_call_target="Cholesky" | custom-call | tf_op jit(solution)/shard_map/jit(cholesky)/cholesky | solution.py:52
  288.1 12.1 %cholesky.465 = f32[128,128]{1,0:T(8,128)S(1)} custom-call(f32[128,128]{1,0:T(8,128)S(1)} %cholesky.603), custom_call_target="Cholesky" | custom-call | tf_op jit(solution)/shard_map/jit(cholesky)/cholesky | solution.py:52
  312.9 11.7 %cholesky.486 = f32[128,128]{1,0:T(8,128)S(1)} custom-call(f32[128,128]{1,0:T(8,128)S(1)} %cholesky.608), custom_call_target="Cholesky" | custom-call | tf_op jit(solution)/shard_map/jit(cholesky)/cholesky | solution.py:52
  336.6 11.9 %cholesky.503 = f32[128,128]{1,0:T(8,128)S(1)} custom-call(f32[128,128]{1,0:T(8,128)S(1)} %convolution_subtract_fusion.14), custom_call_target="Cholesky" | custom-call | tf_op jit(solution)/shard_map/jit(cholesky)/cholesky | solution.py:52
  352.9 11.4 %while.7 = (s32[]{:T(128)}, f32[512,512]{1,0:T(8,128)}, s32[4,2]{0,1:T(2,128)S(1)}, f32[4,128,128]{2,1,0:T(8,128)S(1)}, s32[]{:T(128)}) while((s32[]{:T(128)}, f32[512,512]{1,0:T(8,128)}, s32[4,2]{0,1:T(2,128)S(1)}, f32[4,128,128]{2,1,0:T(8,128)S(1)}, s32[]{:T(128)}) %tuple.105), condition=%wide.while_cond.clone, body=%wide.while_body.clone.sunk | while | flops 2 | bytes 131181 | solution.py:53
  364.3 39.3 %custom-call.42 = f32[4,128,128]{1,2,0:T(8,128)S(1)} custom-call(f32[4,128,128]{2,1,0:T(8,128)S(1)} %get-tuple-element.27), custom_call_target="InvertDiagBlocksLowerTriangular" | custom-call | tf_op jit(solution)/shard_map/jit(_solve_triangular)/triangular_solve | solution.py:53
  425.7 94.6 %all-gather.11.cloned.1.call-done = bf16[32,128,1024]{2,1,0:T(8,128)(2,1)} async-done(((bf16[1,128,1024]{2,1,0:T(8,128)(2,1)}), bf16[32,128,1024]{2,1,0:T(8,128)(2,1)}) %all-gather.11.cloned.1.call-update) | async-done | bytes 8388624 | tf_op jit(solution)/shard_map/all_gather | solution.py:74
  538.0 10.3 %reshape.264 = f32[32,128,512]{2,1,0:T(8,128)} reshape(f32[32,1,128,4,128]{4,3,2,0,1:T(4,128)} %fusion.4) | data formatting | bytes 16777216 | tf_op jit(solution)/shard_map/reshape.65
  548.2 10.4 %fusion.2 = f32[4,128,512]{2,0,1:T(4,128)S(1)} fusion(f32[32,128,512]{2,1,0:T(8,128)} %reshape.264, s32[32]{0:T(128)S(1)} %get-tuple-element.112, pred[32]{0:T(512)(128)(4,1)S(1)} %broadcast_compare_fusion), kind=kOutput, calls=%fused_computation.8 | convolution fusion | flops 100663552 | bytes 9437344 | tf_op jit(solution)/shard_map/muvx,mut->tvx/dot_general | solution.py:34
  565.5 24.5 %all-gather.13.cloned.1.call-done = f32[1,1024,512]{1,2,0:T(8,128)} async-done(((f32[1,128,512]{1,2,0:T(8,128)}), f32[1,1024,512]{1,2,0:T(8,128)}) %all-gather.13.cloned.1.call-update) | async-done | bytes 2097168 | tf_op jit(solution)/shard_map/all_gather | solution.py:79
  593.1 11.7 %cholesky.518 = f32[128,128]{1,0:T(8,128)S(1)} custom-call(f32[128,128]{1,0:T(8,128)S(1)} %cholesky.612), custom_call_target="Cholesky" | custom-call | tf_op jit(solution)/shard_map/jit(cholesky)/cholesky | solution.py:80
  615.5 11.7 %cholesky.537 = f32[128,128]{1,0:T(8,128)S(1)} custom-call(f32[128,128]{1,0:T(8,128)S(1)} %cholesky.616), custom_call_target="Cholesky" | custom-call | tf_op jit(solution)/shard_map/jit(cholesky)/cholesky | solution.py:80
  628.6 10.0 %custom-call.44 = f32[1,128,128]{1,2,0:T(8,128)S(1)} custom-call(f32[1,128,128]{2,1,0:T(8,128)S(1)} %get-tuple-element.80), custom_call_target="InvertDiagBlocksLowerTriangular" | custom-call | tf_op jit(solution)/shard_map/jit(cholesky)/cholesky | solution.py:80
  639.2 11.7 %cholesky.558 = f32[128,128]{1,0:T(8,128)S(1)} custom-call(f32[128,128]{1,0:T(8,128)S(1)} %cholesky.621), custom_call_target="Cholesky" | custom-call | tf_op jit(solution)/shard_map/jit(cholesky)/cholesky | solution.py:80
  662.0 11.9 %cholesky.575 = f32[128,128]{1,0:T(8,128)S(1)} custom-call(f32[128,128]{1,0:T(8,128)S(1)} %convolution_subtract_fusion.13), custom_call_target="Cholesky" | custom-call | tf_op jit(solution)/shard_map/jit(cholesky)/cholesky | solution.py:80
  685.9 39.3 %custom-call.27 = f32[4,128,128]{1,2,0:T(8,128)S(1)} custom-call(f32[4,128,128]{2,1,0:T(8,128)S(1)} %get-tuple-element.19), custom_call_target="InvertDiagBlocksLowerTriangular" | custom-call | tf_op jit(solution)/shard_map/jit(_solve_triangular)/triangular_solve | solution.py:82
  (208 shorter events, 236.9 us)
Async XLA Ops:
  7.2 42.2 %all-gather.7.cloned.1.call-start = ((), (), s32[]{:S(2)}) async-start(), calls=%async_computation | async-start | bytes 4718592 | tf_op jit(solution)/shard_map/all_gather | solution.py:48
  9.1 238.2 %all-gather.9.cloned.1.call-start = ((), (), s32[]{:S(2)}) async-start(), calls=%async_computation.1 | async-start | bytes 4718592 | tf_op jit(solution)/shard_map/all_gather | solution.py:48
  58.9 1.9 copy-start
  193.8 5.7 copy-start.1
  206.0 1.6 copy-start.8
  207.4 5.1 copy-start.4
  212.5 307.8 %all-gather.11.cloned.1.call-start = ((), (), s32[]{:S(2)}) async-start(), calls=%async_computation.2 | async-start | bytes 8650752 | tf_op jit(solution)/shard_map/all_gather | solution.py:74
  256.9 1.9 copy-start.2
  262.9 1.0 copy-start.7
  403.6 5.8 copy-start.3
  418.8 2.4 copy-start.6
  418.9 3.7 copy-start.9
  419.2 5.0 copy-start.10
  419.2 5.0 copy-start.11
  419.3 6.3 copy-start.12
  422.5 167.6 %all-gather.13.cloned.1.call-start = ((), (), s32[]{:S(2)}) async-start(), calls=%async_computation.3 | async-start | bytes 2359296 | tf_op jit(solution)/shard_map/all_gather | solution.py:79
  558.7 3.5 copy-start.5
Sparse Core Ops, SparseCore 0:
  10.4 38.8 all-gather.6
  212.6 34.6 all-gather.8
  422.6 97.6 all-gather.10
  562.3 27.6 all-gather.12
where the time goes:
time: 747 us; the launch traced here: 737 us
  other arithmetic  369 us (49%)
  waiting for transfers between devices  193 us (26%)
  local copies, waits for them, and re-layouts  90.3 us (12%)
  matrix products  61.6 us (8%)
  between operations  22.8 us (3%)
    another operation x29, other arithmetic, on_device(): pivot_block = jnp.linalg.cholesky(gathered[first_col:trailing])  159 us
    all_gather x1, waiting for transfers between devices, on_device(): lax.all_gather(contribution[None], 'leaf', axis=0, tiled=True)  94.6 us
    another operation x5, other arithmetic, on_device(): jax.scipy.linalg.solve_triangular(pivot_block, gathered.T, lower=True)  79.9 us
    another operation x15, other arithmetic, on_device(): pivot_block = jnp.linalg.cholesky(stacked[:PANEL])  79.4 us
    all_gather x2, waiting for transfers between devices, on_device(): lax.all_gather(column.reshape(row_slots, 1, BLK, PANEL), 'panel', axis=1,...  73.8 us
    another operation x2, other arithmetic, on_device(): jax.scipy.linalg.solve_triangular(pivot_block, parent_rows.T, lower=True)  39.4 us
    unnamed x34, local copies, waits for them, and re-layouts  27 us
    all_gather x1, waiting for transfers between devices, on_device(): stacked = lax.all_gather(assembled[0], 'panel', axis=0, tiled=True)  24.5 us
  transfers between devices with their start and end apart: 4, of which 4 were waited for; matrix products, arithmetic and copies ran while one was open for 1% of the time, Pallas kernels for 0%

commit v1 on v0

--- a/solution.py
+++ b/solution.py
@@ -45,8 +45,14 @@
     for first_col in range(0, PC, PANEL):
         trailing = first_col + PANEL
         column = local_rows[:, first_col:trailing]
-        gathered = lax.all_gather(
-            column.reshape(row_slots, 1, BLK, PANEL), "panel", axis=1, tiled=True
+        gathered = jnp.concatenate(
+            lax.all_to_all(
+                jnp.stack([column.reshape(row_slots, 1, BLK, PANEL)] * lax.axis_size("panel")),
+                "panel",
+                0,
+                0,
+            ),
+            axis=1,
         )
         gathered = gathered.reshape(WC, PANEL)
         pivot_block = jnp.linalg.cholesky(gathered[first_col:trailing])

time: 747 us -> 786 us (1.052)
  waiting for transfers between devices: 193 us -> 216 us
  starting transfers between devices: 0.16 us -> 13 us
    all_to_all x0 -> x2, waiting for transfers between devices: none -> 96.8 us  [on_device(): lax.all_to_all(jnp.stack([column.reshape(row_slots, 1, BLK, PANEL)] * lax...]
    all_gather x2 -> x0, waiting for transfers between devices: 73.8 us -> none  [on_device(): lax.all_gather(column.reshape(row_slots, 1, BLK, PANEL), 'panel', axis=1,...]
    another operation x13 -> x19, local copies, waits for them, and re-layouts: 18.7 us -> 35.5 us
    reshape x0 -> x2, local copies, waits for them, and re-layouts: none -> 13.2 us  [on_device(): jnp.concatenate(lax.all_to_all(jnp.stack([column.reshape(row_slots, 1, BL...]
    all_to_all x0 -> x2, starting transfers between devices: none -> 12.9 us  [on_device(): lax.all_to_all(jnp.stack([column.reshape(row_slots, 1, BLK, PANEL)] * lax...]
    unnamed x34 -> x28, local copies, waits for them, and re-layouts: 27 us -> 14.8 us
    all_gather x2 -> x0, local copies, waits for them, and re-layouts: 10.9 us -> none  [on_device(): lax.all_gather(column.reshape(row_slots, 1, BLK, PANEL), 'panel', axis=1,...]
where the time goes in v1:
time: 786 us; the launch traced here: 780 us
  other arithmetic  368 us (47%)
  waiting for transfers between devices  216 us (27%)
  local copies, waits for them, and re-layouts  98.1 us (12%)
  matrix products  61.6 us (8%)
  between operations  23 us (3%)
  starting transfers between devices  13 us (2%)
    another operation x29, other arithmetic, on_device(): pivot_block = jnp.linalg.cholesky(gathered[first_col:trailing])  158 us
    all_to_all x2, waiting for transfers between devices, on_device(): lax.all_to_all(jnp.stack([column.reshape(row_slots, 1, BLK, PANEL)] * lax...  96.8 us
    all_gather x1, waiting for transfers between devices, on_device(): lax.all_gather(contribution[None], 'leaf', axis=0, tiled=True)  94.5 us
    another operation x5, other arithmetic, on_device(): jax.scipy.linalg.solve_triangular(pivot_block, gathered.T, lower=True)  80.2 us
    another operation x15, other arithmetic, on_device(): pivot_block = jnp.linalg.cholesky(stacked[:PANEL])  79.4 us
    another operation x2, other arithmetic, on_device(): jax.scipy.linalg.solve_triangular(pivot_block, parent_rows.T, lower=True)  39.4 us
    all_gather x1, waiting for transfers between devices, on_device(): stacked = lax.all_gather(assembled[0], 'panel', axis=0, tiled=True)  24.5 us
    another operation x14, matrix products, on_device(): jax.scipy.linalg.solve_triangular(pivot_block, gathered.T, lower=True)  24 us
  transfers between devices with their start and end apart: 4, of which 4 were waited for; matrix products, arithmetic and copies ran while one was open for 1% of the time, Pallas kernels for 0%

profile of v1, /device:TPU:1, one launch (start us, length us, event | category | flops | bytes accessed | tf_op | source)
XLA Modules:
  0.0 780.3 jit_solution(2685522328373855479)
XLA Ops:
  19.2 48.9 %all-to-all-done = f32[8,2,1,128,512]{3,1,4,2,0:T(2,128)} async-done(((f32[8,2,1,128,512]{3,1,4,2,0:T(2,128)}), f32[8,2,1,128,512]{3,1,4,2,0:T(2,128)}, u32[]{:S(2)}, u32[]{:S(2)}) %all-to-all-start) | async-done | bytes 4194336 | tf_op jit(solution)/shard_map/all_to_all | solution.py:49
  83.2 11.7 %cholesky.374 = f32[128,128]{1,0:T(8,128)S(1)} custom-call(f32[128,128]{1,0:T(8,128)S(1)} %cholesky.586), custom_call_target="Cholesky" | custom-call | tf_op jit(solution)/shard_map/jit(cholesky)/cholesky | solution.py:58
  105.6 11.7 %cholesky.393 = f32[128,128]{1,0:T(8,128)S(1)} custom-call(f32[128,128]{1,0:T(8,128)S(1)} %cholesky.590), custom_call_target="Cholesky" | custom-call | tf_op jit(solution)/shard_map/jit(cholesky)/cholesky | solution.py:58
  117.3 10.0 %custom-call.36 = f32[1,128,128]{1,2,0:T(8,128)S(1)} custom-call(f32[1,128,128]{2,1,0:T(8,128)S(1)} %get-tuple-element.96), custom_call_target="InvertDiagBlocksLowerTriangular" | custom-call | tf_op jit(solution)/shard_map/jit(cholesky)/cholesky | solution.py:58
  127.9 11.7 %cholesky.414 = f32[128,128]{1,0:T(8,128)S(1)} custom-call(f32[128,128]{1,0:T(8,128)S(1)} %cholesky.595), custom_call_target="Cholesky" | custom-call | tf_op jit(solution)/shard_map/jit(cholesky)/cholesky | solution.py:58
  150.8 11.7 %cholesky.431 = f32[128,128]{1,0:T(8,128)S(1)} custom-call(f32[128,128]{1,0:T(8,128)S(1)} %convolution_subtract_fusion.15), custom_call_target="Cholesky" | custom-call | tf_op jit(solution)/shard_map/jit(cholesky)/cholesky | solution.py:58
  174.9 39.3 %custom-call.38 = f32[4,128,128]{1,2,0:T(8,128)S(1)} custom-call(f32[4,128,128]{2,1,0:T(8,128)S(1)} %get-tuple-element.26), custom_call_target="InvertDiagBlocksLowerTriangular" | custom-call | tf_op jit(solution)/shard_map/jit(_solve_triangular)/triangular_solve | solution.py:59
  241.8 47.8 %all-to-all-done.1 = f32[8,2,1,128,512]{3,1,4,2,0:T(2,128)} async-done(((f32[8,2,1,128,512]{3,1,4,2,0:T(2,128)}), f32[8,2,1,128,512]{3,1,4,2,0:T(2,128)}, u32[]{:S(2)}, u32[]{:S(2)}) %all-to-all-start.1) | async-done | bytes 4194336 | tf_op jit(solution)/shard_map/all_to_all | solution.py:49
  307.4 11.7 %cholesky.446 = f32[128,128]{1,0:T(8,128)S(1)} custom-call(f32[128,128]{1,0:T(8,128)S(1)} %cholesky.599), custom_call_target="Cholesky" | custom-call | tf_op jit(solution)/shard_map/jit(cholesky)/cholesky | solution.py:58
  331.6 11.7 %cholesky.465 = f32[128,128]{1,0:T(8,128)S(1)} custom-call(f32[128,128]{1,0:T(8,128)S(1)} %cholesky.603), custom_call_target="Cholesky" | custom-call | tf_op jit(solution)/shard_map/jit(cholesky)/cholesky | solution.py:58
  344.6 10.2 %custom-call.40 = f32[1,128,128]{1,2,0:T(8,128)S(1)} custom-call(f32[1,128,128]{2,1,0:T(8,128)S(1)} %get-tuple-element.86), custom_call_target="InvertDiagBlocksLowerTriangular" | custom-call | tf_op jit(solution)/shard_map/jit(cholesky)/cholesky | solution.py:58
  356.4 11.7 %cholesky.486 = f32[128,128]{1,0:T(8,128)S(1)} custom-call(f32[128,128]{1,0:T(8,128)S(1)} %cholesky.608), custom_call_target="Cholesky" | custom-call | tf_op jit(solution)/shard_map/jit(cholesky)/cholesky | solution.py:58
  380.2 11.7 %cholesky.503 = f32[128,128]{1,0:T(8,128)S(1)} custom-call(f32[128,128]{1,0:T(8,128)S(1)} %convolution_subtract_fusion.14), custom_call_target="Cholesky" | custom-call | tf_op jit(solution)/shard_map/jit(cholesky)/cholesky | solution.py:58
  396.4 11.4 %while.7 = (s32[]{:T(128)}, f32[512,512]{1,0:T(8,128)}, s32[4,2]{0,1:T(2,128)S(1)}, f32[4,128,128]{2,1,0:T(8,128)S(1)}, s32[]{:T(128)}) while((s32[]{:T(128)}, f32[512,512]{1,0:T(8,128)}, s32[4,2]{0,1:T(2,128)S(1)}, f32[4,128,128]{2,1,0:T(8,128)S(1)}, s32[]{:T(128)}) %tuple.97), condition=%wide.while_cond.clone, body=%wide.while_body.clone.sunk | while | flops 2 | bytes 131181 | solution.py:59
  407.7 39.3 %custom-call.42 = f32[4,128,128]{1,2,0:T(8,128)S(1)} custom-call(f32[4,128,128]{2,1,0:T(8,128)S(1)} %get-tuple-element.27), custom_call_target="InvertDiagBlocksLowerTriangular" | custom-call | tf_op jit(solution)/shard_map/jit(_solve_triangular)/triangular_solve | solution.py:59
  469.2 94.5 %all-gather.5.cloned.1.call-done = bf16[32,128,1024]{2,1,0:T(8,128)(2,1)} async-done(((bf16[1,128,1024]{2,1,0:T(8,128)(2,1)}), bf16[32,128,1024]{2,1,0:T(8,128)(2,1)}) %all-gather.5.cloned.1.call-update) | async-done | bytes 8388624 | tf_op jit(solution)/shard_map/all_gather | solution.py:80
  581.4 10.3 %reshape.264 = f32[32,128,512]{2,1,0:T(8,128)} reshape(f32[32,1,128,4,128]{4,3,2,0,1:T(4,128)} %fusion.4) | data formatting | bytes 16777216 | tf_op jit(solution)/shard_map/reshape.65
  591.7 10.4 %fusion.2 = f32[4,128,512]{2,0,1:T(4,128)S(1)} fusion(f32[32,128,512]{2,1,0:T(8,128)} %reshape.264, s32[32]{0:T(128)S(1)} %get-tuple-element.108, pred[32]{0:T(512)(128)(4,1)S(1)} %broadcast_compare_fusion), kind=kOutput, calls=%fused_computation.8 | convolution fusion | flops 100663552 | bytes 9437344 | tf_op jit(solution)/shard_map/muvx,mut->tvx/dot_general | solution.py:34
  609.0 24.5 %all-gather.7.cloned.1.call-done = f32[1,1024,512]{1,2,0:T(8,128)} async-done(((f32[1,128,512]{1,2,0:T(8,128)}), f32[1,1024,512]{1,2,0:T(8,128)}) %all-gather.7.cloned.1.call-update) | async-done | bytes 2097168 | tf_op jit(solution)/shard_map/all_gather | solution.py:85
  636.6 11.7 %cholesky.518 = f32[128,128]{1,0:T(8,128)S(1)} custom-call(f32[128,128]{1,0:T(8,128)S(1)} %cholesky.612), custom_call_target="Cholesky" | custom-call | tf_op jit(solution)/shard_map/jit(cholesky)/cholesky | solution.py:86
  659.0 11.7 %cholesky.537 = f32[128,128]{1,0:T(8,128)S(1)} custom-call(f32[128,128]{1,0:T(8,128)S(1)} %cholesky.616), custom_call_target="Cholesky" | custom-call | tf_op jit(solution)/shard_map/jit(cholesky)/cholesky | solution.py:86
  682.7 11.7 %cholesky.558 = f32[128,128]{1,0:T(8,128)S(1)} custom-call(f32[128,128]{1,0:T(8,128)S(1)} %cholesky.621), custom_call_target="Cholesky" | custom-call | tf_op jit(solution)/shard_map/jit(cholesky)/cholesky | solution.py:86
  705.5 11.9 %cholesky.575 = f32[128,128]{1,0:T(8,128)S(1)} custom-call(f32[128,128]{1,0:T(8,128)S(1)} %convolution_subtract_fusion.13), custom_call_target="Cholesky" | custom-call | tf_op jit(solution)/shard_map/jit(cholesky)/cholesky | solution.py:86
  729.3 39.3 %custom-call.27 = f32[4,128,128]{1,2,0:T(8,128)S(1)} custom-call(f32[4,128,128]{2,1,0:T(8,128)S(1)} %get-tuple-element.19), custom_call_target="InvertDiagBlocksLowerTriangular" | custom-call | tf_op jit(solution)/shard_map/jit(_solve_triangular)/triangular_solve | solution.py:88
  (206 shorter events, 258.0 us)
Async XLA Ops:
  11.5 56.6 %all-to-all-start = ((f32[8,2,1,128,512]{3,1,4,2,0:T(2,128)}), f32[8,2,1,128,512]{3,1,4,2,0:T(2,128)}, u32[]{:S(2)}, u32[]{:S(2)}) async-start(f32[8,2,1,128,512]{3,1,4,2,0:T(2,128)} %stack.6), calls=%async_computation | async-start | bytes 8388608 | tf_op jit(solution)/shard_map/all_to_all | solution.py:49
  214.3 5.8 copy-start
  226.5 1.6 copy-start.6
  227.8 4.3 copy-start.2
  235.4 54.2 %all-to-all-start.1 = ((f32[8,2,1,128,512]{3,1,4,2,0:T(2,128)}), f32[8,2,1,128,512]{3,1,4,2,0:T(2,128)}, u32[]{:S(2)}, u32[]{:S(2)}) async-start(f32[8,2,1,128,512]{3,1,4,2,0:T(2,128)} %stack.7), calls=%async_computation.1 | async-start | bytes 8388608 | tf_op jit(solution)/shard_map/all_to_all | solution.py:49
  240.7 323.0 %all-gather.5.cloned.1.call-start = ((), (), s32[]{:S(2)}) async-start(), calls=%async_computation.2 | async-start | bytes 8650752 | tf_op jit(solution)/shard_map/all_gather | solution.py:80
  306.4 1.0 copy-start.5
  447.1 5.8 copy-start.1
  462.3 2.4 copy-start.4
  462.3 3.7 copy-start.7
  462.7 5.0 copy-start.8
  462.7 5.0 copy-start.9
  462.7 6.3 copy-start.10
  465.9 167.6 %all-gather.7.cloned.1.call-start = ((), (), s32[]{:S(2)}) async-start(), calls=%async_computation.3 | async-start | bytes 2359296 | tf_op jit(solution)/shard_map/all_gather | solution.py:85
  602.1 3.5 copy-start.3
Sparse Core Ops, SparseCore 0:
  466.1 97.6 all-gather.4
  605.8 27.6 all-gather.6
